TPU v7x, 32 devices: a whole 2x2x4 slice. The times are simulated.
32 devices in a mesh: dp: 16 (over z, y, x), head: 2 (over core).
Axes of the slice: x: 2, y: 2, z: 4, core: 2. Of those that a mesh axis runs over, the one named last changes fastest.
Arguments:
- tokens: bfloat16 [8192, 2048], P('dp'), may hold values from -6 to 6
- seq_count: int32 [16], P('dp'), may hold values from 1 to 2
- valid_len: int32 [32], P('dp'), may hold values from 128 to 256
- attn_gain: bfloat16 [2048], P('dp'), may hold values from 0.5 to 1.5
- ffn_gain: bfloat16 [2048], P('dp'), may hold values from 0.5 to 1.5
- q_weight: bfloat16 [2048, 2048], P('dp', 'head'), may hold values from -0.25 to 0.25
- k_weight: bfloat16 [2048, 2048], P('dp', 'head'), may hold values from -0.25 to 0.25
- v_weight: bfloat16 [2048, 2048], P('dp', 'head'), may hold values from -0.125 to 0.125
- forget_weight: bfloat16 [2048, 256], P('dp', 'head'), may hold values from -0.125 to 0.125
- out_weight: bfloat16 [2048, 2048], P('dp', 'head'), may hold values from -1.5 to 1.5
- gate_weight: bfloat16 [2048, 5632], P('dp', 'head'), may hold values from -0.125 to 0.125
- up_weight: bfloat16 [2048, 5632], P('dp', 'head'), may hold values from -0.125 to 0.125
- down_weight: bfloat16 [2048, 5632], P('dp', 'head'), may hold values from -0.078125 to 0.078125
- cotangent: float32 [8192, 2048], P('dp'), may hold values from -6 to 6
Outputs:
- block_out: bfloat16 [8192, 2048], P('dp')
- input_grad: float32 [8192, 2048], P('dp')
- attn_gain_grad: float32 [2048], P('dp')
- ffn_gain_grad: float32 [2048], P('dp')
- q_grad: float32 [2048, 2048], P('dp', 'head')
- k_grad: float32 [2048, 2048], P('dp', 'head')
- v_grad: float32 [2048, 2048], P('dp', 'head')
- forget_grad: float32 [2048, 256], P('dp', 'head')
- out_grad: float32 [2048, 2048], P('dp', 'head')
- gate_grad: float32 [2048, 5632], P('dp', 'head')
- up_grad: float32 [2048, 5632], P('dp', 'head')
- down_grad: float32 [2048, 5632], P('dp', 'head')
All inputs are finite; a program needn't handle non-finite values.
Results may differ from a plain program's by a relative error of at most 0.0089.
Values may be sent and summed in bfloat16 or wider, within the bound.
A program may use at most 256 MiB of HBM per device.

v0:
```python
import jax
import jax.numpy as jnp
from jax import lax
from jax.sharding import PartitionSpec as P

SLOTS = 64
KDIM = 512
SEQ_LEN = 256


def einsum_high(form, left, right):
    return jnp.einsum(form, left, right, precision=lax.Precision.HIGHEST)


def times_trans(left, right):
    return lax.dot_general(
        left, right, (((1,), (1,)), ((), ())), preferred_element_type=jnp.float32
    )


def outer_sum(left, right):
    return lax.dot_general(
        left, right, (((0,), (0,)), ((), ())), preferred_element_type=jnp.float32
    )


def rms_norm(values, gain):
    return values * lax.rsqrt(jnp.mean(values * values, axis=-1, keepdims=True) + 1e-06) * gain


def swiglu(gate_vals, up_vals):
    return jax.nn.silu(gate_vals) * up_vals


def block_step(states, block):
    key_state, value_state = states
    query_block, key_block, value_block, forget_block = block
    width = query_block.shape[0]
    totals = jnp.cumsum(forget_block, axis=0)
    writes = -jnp.expm1(forget_block)
    order = jnp.arange(width, dtype=jnp.int32)
    lower = (order[:, None] >= order[None, :])[:, :, None]
    spread = jnp.where(lower, totals[:, None, :] - totals[None, :, :], 0.0)
    decays = jnp.where(lower, jnp.exp(spread), 0.0) * writes[None, :, :]
    products = einsum_high("td,id->ti", query_block, key_block)
    carried = jnp.exp(totals)
    scores = einsum_high("ti,tim->tm", products, decays) + carried * einsum_high(
        "td,md->tm", query_block, key_state
    )
    weights = jax.nn.softmax(scores, axis=-1)
    mixing = einsum_high("tm,tim->ti", weights, decays)
    result = einsum_high("ti,id->td", mixing, value_block) + einsum_high(
        "tm,md->td", weights * carried, value_state
    )
    final = totals[-1]
    tails = jnp.exp(final[None, :] - totals) * writes
    key_next = jnp.exp(final)[:, None] * key_state + einsum_high("im,id->md", tails, key_block)
    value_next = jnp.exp(final)[:, None] * value_state + einsum_high(
        "im,id->md", tails, value_block
    )
    return ((key_next, value_next), result)


def scan_slots(query, keys, values_in, forget):
    width = min(64, SEQ_LEN)
    count = SEQ_LEN // width
    pieces = (
        query.reshape(count, width, KDIM),
        keys.reshape(count, width, KDIM),
        values_in.reshape(count, width, KDIM),
        forget.reshape(count, width, SLOTS),
    )
    start = (jnp.zeros((SLOTS, KDIM), jnp.float32), jnp.zeros((SLOTS, KDIM), jnp.float32))
    ignored, outputs = lax.scan(jax.checkpoint(block_step), start, pieces)
    return outputs.reshape(SEQ_LEN, KDIM)


def mixer(query_proj, key_proj, value_proj, forget_proj):
    rows = query_proj.shape[0]
    seq_total = rows // SEQ_LEN
    head_total = forget_proj.shape[1] // SLOTS

    def split(values, width):
        shaped = values.reshape(seq_total, SEQ_LEN, head_total, width).transpose(0, 2, 1, 3)
        return shaped.reshape(seq_total * head_total, SEQ_LEN, width)

    query = split(jax.nn.silu(query_proj), KDIM) * KDIM ** (-0.5)
    keys = split(jax.nn.silu(key_proj), KDIM)
    values_in = split(value_proj, KDIM)
    forget = split(jax.nn.log_sigmoid(forget_proj) / 8.0, SLOTS)
    outputs = jax.vmap(scan_slots)(query, keys, values_in, forget)
    outputs = outputs.reshape(seq_total, head_total, SEQ_LEN, KDIM).transpose(0, 2, 1, 3)
    return outputs.reshape(rows, head_total * KDIM)


def body(
    tokens,
    seq_count,
    valid_len,
    attn_gain,
    ffn_gain,
    q_weight,
    k_weight,
    v_weight,
    forget_weight,
    out_weight,
    gate_weight,
    up_weight,
    down_weight,
    cotangent,
):
    shards = (
        attn_gain,
        ffn_gain,
        q_weight,
        k_weight,
        v_weight,
        forget_weight,
        out_weight,
        gate_weight,
        up_weight,
        down_weight,
    )
    whole = (
        lax.all_gather(shards[0], "dp", axis=0, tiled=True),
        lax.all_gather(shards[1], "dp", axis=0, tiled=True),
        lax.all_gather(shards[2], "dp", axis=0, tiled=True),
        lax.all_gather(shards[3], "dp", axis=0, tiled=True),
        lax.all_gather(shards[4], "dp", axis=0, tiled=True),
        lax.all_gather(shards[5], "dp", axis=0, tiled=True),
        lax.all_gather(shards[6], "dp", axis=0, tiled=True),
        lax.all_gather(shards[7], "dp", axis=0, tiled=True),
        lax.all_gather(shards[8], "dp", axis=0, tiled=True),
        lax.all_gather(shards[9], "dp", axis=0, tiled=True),
    )
    gain_attn, gain_ffn, w_query, w_key, w_value, w_forget, w_out, w_gate, w_up, w_down = whole
    rows = tokens.shape[0]
    places = jnp.arange(rows, dtype=jnp.int32)
    slot_ids = places // SEQ_LEN
    inside = places % SEQ_LEN
    slot_range = jnp.arange(valid_len.shape[0], dtype=jnp.int32)
    lengths = jnp.sum(
        jnp.where(slot_ids[:, None] == slot_range[None, :], valid_len[None, :], 0), axis=1
    )
    live = ((slot_ids < seq_count[0]) & (inside < lengths)).astype(jnp.float32)[:, None]
    inputs = tokens.astype(jnp.float32)
    normed_attn, attn_norm_back = jax.vjp(rms_norm, inputs, gain_attn.astype(jnp.float32))
    attn_in = normed_attn.astype(jnp.bfloat16)
    query_proj = jnp.dot(attn_in, w_query, preferred_element_type=jnp.float32)
    key_proj = jnp.dot(attn_in, w_key, preferred_element_type=jnp.float32)
    value_proj = jnp.dot(attn_in, w_value, preferred_element_type=jnp.float32)
    forget_proj = jnp.dot(attn_in, w_forget, preferred_element_type=jnp.float32)
    mixed_full, mixer_back = jax.vjp(mixer, query_proj, key_proj, value_proj, forget_proj)
    mixed = mixed_full.astype(jnp.bfloat16)
    attn = lax.psum(times_trans(mixed, w_out), "head")
    resid = inputs + attn
    normed_ffn, ffn_norm_back = jax.vjp(rms_norm, resid, gain_ffn.astype(jnp.float32))
    ffn_in = normed_ffn.astype(jnp.bfloat16)
    gate_vals = jnp.dot(ffn_in, w_gate, preferred_element_type=jnp.float32)
    up_vals = jnp.dot(ffn_in, w_up, preferred_element_type=jnp.float32)
    hidden_full, glu_back = jax.vjp(swiglu, gate_vals, up_vals)
    hidden = hidden_full.astype(jnp.bfloat16)
    ffn = lax.psum(times_trans(hidden, w_down), "head")
    block_out = (live * (resid + ffn)).astype(jnp.bfloat16)
    again = (
        lax.all_gather(shards[0], "dp", axis=0, tiled=True),
        lax.all_gather(shards[1], "dp", axis=0, tiled=True),
        lax.all_gather(shards[2], "dp", axis=0, tiled=True),
        lax.all_gather(shards[3], "dp", axis=0, tiled=True),
        lax.all_gather(shards[4], "dp", axis=0, tiled=True),
        lax.all_gather(shards[5], "dp", axis=0, tiled=True),
        lax.all_gather(shards[6], "dp", axis=0, tiled=True),
        lax.all_gather(shards[7], "dp", axis=0, tiled=True),
        lax.all_gather(shards[8], "dp", axis=0, tiled=True),
        lax.all_gather(shards[9], "dp", axis=0, tiled=True),
    )
    gain_attn, gain_ffn, w_query, w_key, w_value, w_forget, w_out, w_gate, w_up, w_down = again
    grad_res = live * cotangent
    grad_ffn = grad_res.astype(jnp.bfloat16)
    grad_down = outer_sum(grad_ffn, hidden)
    grad_hidden = jnp.dot(grad_ffn, w_down, preferred_element_type=jnp.float32)
    grad_gate_vals, grad_up_vals = glu_back(grad_hidden)
    gate_low = grad_gate_vals.astype(jnp.bfloat16)
    up_low = grad_up_vals.astype(jnp.bfloat16)
    grad_gate = outer_sum(ffn_in, gate_low)
    grad_up = outer_sum(ffn_in, up_low)
    grad_ffn_in = lax.psum(times_trans(gate_low, w_gate) + times_trans(up_low, w_up), "head")
    grad_resid_norm, grad_gain_ffn = ffn_norm_back(grad_ffn_in)
    grad_resid = grad_res + grad_resid_norm
    grad_attn = grad_resid.astype(jnp.bfloat16)
    grad_out = outer_sum(grad_attn, mixed)
    grad_mixed = jnp.dot(grad_attn, w_out, preferred_element_type=jnp.float32)
    grad_qproj, grad_kproj, grad_vproj, grad_fproj = mixer_back(grad_mixed)
    query_low = grad_qproj.astype(jnp.bfloat16)
    key_low = grad_kproj.astype(jnp.bfloat16)
    value_low = grad_vproj.astype(jnp.bfloat16)
    forget_low = grad_fproj.astype(jnp.bfloat16)
    grad_query = outer_sum(attn_in, query_low)
    grad_key = outer_sum(attn_in, key_low)
    grad_value = outer_sum(attn_in, value_low)
    grad_forget = outer_sum(attn_in, forget_low)
    local_in = (
        times_trans(query_low, w_query)
        + times_trans(key_low, w_key)
        + times_trans(value_low, w_value)
        + times_trans(forget_low, w_forget)
    )
    grad_attn_in = lax.psum(local_in, "head")
    grad_input_norm, grad_gain_attn = attn_norm_back(grad_attn_in)
    input_grad = grad_resid + grad_input_norm
    reduced = (
        lax.psum_scatter(grad_gain_attn, "dp", scatter_dimension=0, tiled=True),
        lax.psum_scatter(grad_gain_ffn, "dp", scatter_dimension=0, tiled=True),
        lax.psum_scatter(grad_query, "dp", scatter_dimension=0, tiled=True),
        lax.psum_scatter(grad_key, "dp", scatter_dimension=0, tiled=True),
        lax.psum_scatter(grad_value, "dp", scatter_dimension=0, tiled=True),
        lax.psum_scatter(grad_forget, "dp", scatter_dimension=0, tiled=True),
        lax.psum_scatter(grad_out, "dp", scatter_dimension=0, tiled=True),
        lax.psum_scatter(grad_gate, "dp", scatter_dimension=0, tiled=True),
        lax.psum_scatter(grad_up, "dp", scatter_dimension=0, tiled=True),
        lax.psum_scatter(grad_down, "dp", scatter_dimension=0, tiled=True),
    )
    return (
        block_out,
        input_grad,
        reduced[0],
        reduced[1],
        reduced[2],
        reduced[3],
        reduced[4],
        reduced[5],
        reduced[6],
        reduced[7],
        reduced[8],
        reduced[9],
    )


def solution(mesh):
    in_specs = (
        P("dp", None),
        P("dp"),
        P("dp"),
        P("dp"),
        P("dp"),
        P("dp", "head"),
        P("dp", "head"),
        P("dp", "head"),
        P("dp", "head"),
        P("dp", "head"),
        P("dp", "head"),
        P("dp", "head"),
        P("dp", "head"),
        P("dp", None),
    )
    out_specs = (
        P("dp", None),
        P("dp", None),
        P("dp"),
        P("dp"),
        P("dp", "head"),
        P("dp", "head"),
        P("dp", "head"),
        P("dp", "head"),
        P("dp", "head"),
        P("dp", "head"),
        P("dp", "head"),
        P("dp", "head"),
    )
    return jax.shard_map(body, mesh=mesh, in_specs=in_specs, out_specs=out_specs, check_vma=False)
```

profile of v0, /device:TPU:10, one launch (start us, length us, event | category | flops | bytes accessed | tf_op | source)
XLA Modules:
  0.0 3717.7 jit_solution(2996730783707626634)
XLA Ops:
  14.0 35.8 all_gather.39
  49.8 40.5 %all-gather = bf16[16,1,128]{2,1,0:T(2,128)(2,1)S(1)} all-gather(bf16[1,1,128]{2,1,0:T(2,128)(2,1)S(1)} %bitcast.437), channel_id=1, replica_groups=mesh['dp'=16,'head'=2] {'dp'}, dimensions={0}, use_global_device_ids=true | all-gather | bytes 4352 | tf_op jit(solution)/shard_map/all_gather | solution.py:125
  110.8 57.6 %all-gather.12.cloned.1.call-done = bf16[2048,1024]{1,0:T(8,128)(2,1)} async-done(((bf16[128,1024]{1,0:T(8,128)(2,1)}), bf16[2048,1024]{1,0:T(8,128)(2,1)}) %all-gather.12.cloned.1.call-update) | async-done | bytes 4194320 | tf_op jit(solution)/shard_map/all_gather | solution.py:129
  181.9 64.0 %all-gather.14.cloned.1.call-done = bf16[2048,1024]{1,0:T(8,128)(2,1)} async-done(((bf16[128,1024]{1,0:T(8,128)(2,1)}), bf16[2048,1024]{1,0:T(8,128)(2,1)}) %all-gather.14.cloned.1.call-update) | async-done | bytes 4194320 | tf_op jit(solution)/shard_map/all_gather | solution.py:127
  260.2 175.8 %while.48 = (s32[]{:T(128)}, f32[4,64,512]{2,1,0:T(8,128)S(1)}, f32[4,64,512]{2,1,0:T(8,128)S(1)}, bf16[4,4,64,512]{3,2,0,1:T(8,128)(2,1)}, f32[4,4,64,512]{3,2,...) while((s32[]{:T(128)}, f32[4,64,512]{2,1,0:T(8,128)S(1)}, ...), condition=%wide.region_6.7_spmd.clone.clone, body=%wide.region_2.6_spmd.clone.clone.sunk | while | flops 640237632 | bytes 21779780 | solution.py:74
  284.2 15.7 fusion.406
  328.0 15.7 fusion.406
  371.8 15.7 fusion.406
  415.6 15.7 fusion.406
  447.7 29.5 all-gather.1
  483.3 133.9 %all-gather.18.cloned.1.call-done = bf16[2048,2816]{1,0:T(8,128)(2,1)} async-done(((bf16[128,2816]{1,0:T(8,128)(2,1)}), bf16[2048,2816]{1,0:T(8,128)(2,1)}) %all-gather.18.cloned.1.call-update) | async-done | bytes 11534352 | tf_op jit(solution)/shard_map/all_gather | solution.py:132
  628.5 132.2 %all-gather.20.cloned.1.call-done = bf16[2048,2816]{1,0:T(8,128)(2,1)} async-done(((bf16[128,2816]{1,0:T(8,128)(2,1)}), bf16[2048,2816]{1,0:T(8,128)(2,1)}) %all-gather.20.cloned.1.call-update) | async-done | bytes 11534352 | tf_op jit(solution)/shard_map/all_gather | solution.py:133
  771.8 132.4 %all-gather.22.cloned.1.call-done = bf16[2048,2816]{1,0:T(8,128)(2,1)} async-done(((bf16[128,2816]{1,0:T(8,128)(2,1)}), bf16[2048,2816]{1,0:T(8,128)(2,1)}) %all-gather.22.cloned.1.call-update) | async-done | bytes 11534352 | tf_op jit(solution)/shard_map/all_gather | solution.py:134
  904.2 16.3 multiply_convert_fusion
  953.7 17.6 all-reduce.11.cloned.1.call-done
  995.3 389.0 %while.47 = (s32[]{:T(128)}, f32[4,64,512]{2,1,0:T(8,128)S(1)}, f32[4,64,512]{2,1,0:T(8,128)}, f32[4,4,64,512]{3,2,0,1:T(8,128)}, f32[4,4,64,512]{3,2,0,1:T(8,12...) while((s32[]{:T(128)}, f32[4,64,512]{2,1,0:T(8,128)S(1)}, ...), condition=%wide.region_24.25_spmd.clone, body=%wide.region_12.24_spmd.clone.sunk | while | flops 1495470592 | bytes 52910904 | solution.py:74
  1043.2 15.4 fusion.380
  1063.1 14.9 fusion.385
  1138.6 15.4 fusion.380
  1158.2 15.1 fusion.385
  1233.9 15.4 fusion.380
  1253.6 14.9 fusion.385
  1329.1 15.4 fusion.380
  1349.0 14.9 fusion.385
  1492.0 71.4 %all-reduce.3 = (f32[2048]{0:T(1024)S(1)}, f32[2048]{0:T(1024)S(1)}) all-reduce(f32[2048]{0:T(1024)S(1)} %get-tuple-element.678, f32[2048]{0:T(1024)S(1)} %copy-done.49), channel_id=2, replica_groups=mesh['dp'=16,'head'=2] {'dp'}, use_global_device_ids=true, to_apply=%region_28.29.clone | all-reduce | flops 4096 | bytes 32768
  1574.0 139.0 %reduce-scatter.9.cloned.1.call-done = f32[128,1024]{1,0:T(8,128)} async-done(((f32[2048,1024]{1,0:T(8,128)}), f32[128,1024]{1,0:T(8,128)}) %reduce-scatter.9.cloned.1.call-update) | async-done | bytes 524304 | tf_op jit(solution)/shard_map/reduce_scatter | solution.py:214
  1713.0 184.0 %reduce-scatter.11.cloned.1.call-done = f32[128,1024]{1,0:T(8,128)} async-done(((f32[2048,1024]{1,0:T(8,128)}), f32[128,1024]{1,0:T(8,128)}) %reduce-scatter.11.cloned.1.call-update) | async-done | bytes 524304 | tf_op jit(solution)/shard_map/reduce_scatter | solution.py:215
  1897.1 183.1 %reduce-scatter.13.cloned.1.call-done = f32[128,1024]{1,0:T(8,128)} async-done(((f32[2048,1024]{1,0:T(8,128)}), f32[128,1024]{1,0:T(8,128)}) %reduce-scatter.13.cloned.1.call-update) | async-done | bytes 524304 | tf_op jit(solution)/shard_map/reduce_scatter | solution.py:216
  2080.2 183.1 %reduce-scatter.17.cloned.1.call-done = f32[128,1024]{1,0:T(8,128)} async-done(((f32[2048,1024]{1,0:T(8,128)}), f32[128,1024]{1,0:T(8,128)}) %reduce-scatter.17.cloned.1.call-update) | async-done | bytes 524304 | tf_op jit(solution)/shard_map/reduce_scatter | solution.py:218
  2263.3 482.0 %reduce-scatter.19.cloned.1.call-done = f32[128,2816]{1,0:T(8,128)} async-done(((f32[2048,2816]{1,0:T(8,128)}), f32[128,2816]{1,0:T(8,128)}) %reduce-scatter.19.cloned.1.call-update) | async-done | bytes 1441808 | tf_op jit(solution)/shard_map/reduce_scatter | solution.py:219
  2745.2 482.7 %reduce-scatter.21.cloned.1.call-done = f32[128,2816]{1,0:T(8,128)} async-done(((f32[2048,2816]{1,0:T(8,128)}), f32[128,2816]{1,0:T(8,128)}) %reduce-scatter.21.cloned.1.call-update) | async-done | bytes 1441808 | tf_op jit(solution)/shard_map/reduce_scatter | solution.py:220
  3227.9 482.7 %reduce-scatter.23.cloned.1.call-done = f32[128,2816]{1,0:T(8,128)} async-done(((f32[2048,2816]{1,0:T(8,128)}), f32[128,2816]{1,0:T(8,128)}) %reduce-scatter.23.cloned.1.call-update) | async-done | bytes 1441808 | tf_op jit(solution)/shard_map/reduce_scatter | solution.py:221
  (689 shorter events, 636.2 us)
Async XLA Ops:
  7.2 42.6 %copy-start.56 = (bf16[128]{0:T(256)(128)(2,1)S(1)}, bf16[128]{0:T(256)(128)(2,1)}, u32[]{:S(2)}) copy-start(bf16[128]{0:T(256)(128)(2,1)} %param.21) | copy-start | bytes 772
  7.2 83.1 %copy-start.5 = (bf16[512,2048]{1,0:T(8,128)(2,1)S(1)}, bf16[512,2048]{1,0:T(8,128)(2,1)}, u32[]{:S(2)}) copy-start(bf16[512,2048]{1,0:T(8,128)(2,1)} %param.18) | copy-start | bytes 6291460
  7.2 89.1 %all-gather.10.cloned.1.call-start = ((), (), s32[]{:S(2)}) async-start(), calls=%async_computation.8 | async-start | bytes 4456448 | tf_op jit(solution)/shard_map/all_gather | solution.py:128
  7.9 160.5 %all-gather.12.cloned.1.call-start = ((), (), s32[]{:S(2)}) async-start(), calls=%async_computation.9 | async-start | bytes 4456448 | tf_op jit(solution)/shard_map/all_gather | solution.py:129
  8.7 237.2 %all-gather.14.cloned.1.call-start = ((), (), s32[]{:S(2)}) async-start(), calls=%async_computation.10 | async-start | bytes 4456448 | tf_op jit(solution)/shard_map/all_gather | solution.py:127
  9.4 429.2 %all-gather.16.cloned.1.call-start = ((), (), s32[]{:S(2)}) async-start(), calls=%async_computation.11 | async-start | bytes 4456448 | tf_op jit(solution)/shard_map/all_gather | solution.py:131
  10.0 468.0 %all-reduce.9.cloned.1.call-start = ((), (), s32[]{:S(2)}) async-start(), calls=%async_computation.12 | async-start | bytes 8388608 | tf_op jit(solution)/shard_map/psum | solution.py:155
  49.8 41.0 %copy-start.36 = (bf16[2048,128]{1,0:T(8,128)(2,1)}, bf16[2048,128]{1,0:T(8,128)(2,1)S(1)}, u32[]{:S(2)}) copy-start(bf16[2048,128]{1,0:T(8,128)(2,1)S(1)} %all_gather.39) | copy-start | bytes 1572868
  90.3 155.6 %copy-start.46 = (f32[16,1,128]{2,1,0:T(1,128)}, f32[16,1,128]{2,1,0:T(1,128)S(1)}, u32[]{:S(2)}) copy-start(f32[16,1,128]{2,1,0:T(1,128)S(1)} %convert_element_type.104) | copy-start | bytes 24580
  90.8 155.1 %copy-start.50 = (f32[512]{0:T(512)}, f32[512]{0:T(512)S(1)}, u32[]{:S(2)}) copy-start(f32[512]{0:T(512)S(1)} %fusion.151) | copy-start | bytes 6148
  284.2 17.4 copy-start.25
  371.8 17.4 copy-start.25
  415.6 17.3 copy-start.25
  445.6 32.3 copy-start.58
  445.6 171.6 %all-gather.18.cloned.1.call-start = ((), (), s32[]{:S(2)}) async-start(), calls=%async_computation.13 | async-start | bytes 12255232 | tf_op jit(solution)/shard_map/all_gather | solution.py:132
  446.2 314.5 %all-gather.20.cloned.1.call-start = ((), (), s32[]{:S(2)}) async-start(), calls=%async_computation.14 | async-start | bytes 12255232 | tf_op jit(solution)/shard_map/all_gather | solution.py:133
  446.9 457.3 %all-gather.22.cloned.1.call-start = ((), (), s32[]{:S(2)}) async-start(), calls=%async_computation.15 | async-start | bytes 12255232 | tf_op jit(solution)/shard_map/all_gather | solution.py:134
  447.7 523.6 %all-reduce.11.cloned.1.call-start = ((), (), s32[]{:S(2)}) async-start(), calls=%async_computation.16 | async-start | bytes 8388608 | tf_op jit(solution)/shard_map/psum | solution.py:187
  478.0 498.5 %copy-start.52 = (f32[512]{0:T(512)}, f32[512]{0:T(512)S(1)}, u32[]{:S(2)}) copy-start(f32[512]{0:T(512)S(1)} %and_convert_fusion) | copy-start | bytes 6148
  483.3 277.4 %copy-start.35 = (bf16[512,2048]{1,0:T(8,128)(2,1)}, bf16[512,2048]{1,0:T(8,128)(2,1)S(1)}, u32[]{:S(2)}) copy-start(bf16[512,2048]{1,0:T(8,128)(2,1)S(1)} %multiply_convert_fusion.3) | copy-start | bytes 6291460
  904.2 28.7 slice-start
  904.2 28.7 slice-start.1
  942.2 546.3 %all-reduce.13.cloned.1.call-start = ((), (), s32[]{:S(2)}) async-start(), calls=%async_computation.25 | async-start | bytes 16777216 | tf_op jit(solution)/shard_map/psum | solution.py:163
  1410.5 163.5 %reduce-scatter.15.cloned.1.call-start = ((), (), s32[]{:S(2)}) async-start(), calls=%async_computation.20 | async-start | bytes 1114112 | tf_op jit(solution)/shard_map/reduce_scatter | solution.py:217
  1414.1 298.9 %reduce-scatter.9.cloned.1.call-start = ((), (), s32[]{:S(2)}) async-start(), calls=%async_computation.17 | async-start | bytes 8912896 | tf_op jit(solution)/shard_map/reduce_scatter | solution.py:214
  1422.0 475.1 %reduce-scatter.11.cloned.1.call-start = ((), (), s32[]{:S(2)}) async-start(), calls=%async_computation.18 | async-start | bytes 8912896 | tf_op jit(solution)/shard_map/reduce_scatter | solution.py:215
  1428.2 651.9 %reduce-scatter.13.cloned.1.call-start = ((), (), s32[]{:S(2)}) async-start(), calls=%async_computation.19 | async-start | bytes 8912896 | tf_op jit(solution)/shard_map/reduce_scatter | solution.py:216
  1435.3 827.9 %reduce-scatter.17.cloned.1.call-start = ((), (), s32[]{:S(2)}) async-start(), calls=%async_computation.21 | async-start | bytes 8912896 | tf_op jit(solution)/shard_map/reduce_scatter | solution.py:218
  1445.6 1299.6 %reduce-scatter.19.cloned.1.call-start = ((), (), s32[]{:S(2)}) async-start(), calls=%async_computation.22 | async-start | bytes 24510464 | tf_op jit(solution)/shard_map/reduce_scatter | solution.py:219
  1459.3 1768.5 %reduce-scatter.21.cloned.1.call-start = ((), (), s32[]{:S(2)}) async-start(), calls=%async_computation.23 | async-start | bytes 24510464 | tf_op jit(solution)/shard_map/reduce_scatter | solution.py:220
  1472.5 2238.1 %reduce-scatter.23.cloned.1.call-start = ((), (), s32[]{:S(2)}) async-start(), calls=%async_computation.24 | async-start | bytes 24510464 | tf_op jit(solution)/shard_map/reduce_scatter | solution.py:221
  1486.6 78.0 %copy-start.55 = (f32[512]{0:T(512)S(1)}, f32[512]{0:T(512)}, u32[]{:S(2)}) copy-start(f32[512]{0:T(512)} %copy-done.54) | copy-start | bytes 6148
  (133 other events, 1011.4 us)
Sparse Core Ops, SparseCore 0:
  10.8 80.0 all-gather.9
  93.6 74.7 all-gather.11
  171.2 74.6 all-gather.13
  248.5 74.6 all-gather.15
  445.7 27.3 all-reduce.8
  476.1 141.0 all-gather.17
  620.3 140.3 all-gather.19
  763.8 140.3 all-gather.21
  942.3 28.9 all-reduce.10
  1410.7 40.1 all-reduce.12
  1453.7 67.9 reduce-scatter.14
  1524.5 188.5 reduce-scatter.8
  1716.0 181.0 reduce-scatter.10
  1899.9 180.2 reduce-scatter.12
  2083.0 180.2 reduce-scatter.16
  2266.1 479.0 reduce-scatter.18
  2748.1 479.7 reduce-scatter.20
  3230.7 479.7 reduce-scatter.22
where the time goes:
time: 3730 us; the launch traced here: 3720 us
  waiting for transfers between devices  2680 us (72%)
  matrix products  590 us (16%)
  blocking collectives  177 us (5%)
  local copies, waits for them, and re-layouts  127 us (3%)
  other arithmetic  114 us (3%)
    reduce_scatter x1, waiting for transfers between devices, body(): lax.psum_scatter(grad_down, 'dp', scatter_dimension=0, tiled=True)  483 us
    reduce_scatter x1, waiting for transfers between devices, body(): lax.psum_scatter(grad_up, 'dp', scatter_dimension=0, tiled=True)  483 us
    reduce_scatter x1, waiting for transfers between devices, body(): lax.psum_scatter(grad_gate, 'dp', scatter_dimension=0, tiled=True)  482 us
    dot_general x104, matrix products, einsum_high(): return jnp.einsum(form, left, right, precision=lax.Precision.HIGHEST)  406 us
    reduce_scatter x1, waiting for transfers between devices, body(): lax.psum_scatter(grad_key, 'dp', scatter_dimension=0, tiled=True)  184 us
    reduce_scatter x1, waiting for transfers between devices, body(): lax.psum_scatter(grad_value, 'dp', scatter_dimension=0, tiled=True)  183 us
    reduce_scatter x1, waiting for transfers between devices, body(): lax.psum_scatter(grad_out, 'dp', scatter_dimension=0, tiled=True)  183 us
    reduce_scatter x1, waiting for transfers between devices, body(): lax.psum_scatter(grad_query, 'dp', scatter_dimension=0, tiled=True)  139 us
  transfers between devices with their start and end apart: 18, of which 13 were waited for; matrix products, arithmetic and copies ran while one was open for 9% of the time, Pallas kernels for 0%

commit v1 on v0

--- a/solution.py
+++ b/solution.py
@@ -6,6 +6,18 @@
 SLOTS = 64
 KDIM = 512
 SEQ_LEN = 256
+
+
+def doubled_up(value, axis, dim):
+    ways, here = (lax.axis_size(axis), lax.axis_index(axis))
+    grown, reach = (value, 1)
+    while reach < ways:
+        theirs = lax.ppermute(grown, axis, [(d, d ^ reach) for d in range(ways)])
+        mine_first = jnp.concatenate([grown, theirs], axis=dim)
+        theirs_first = jnp.concatenate([theirs, grown], axis=dim)
+        grown = jnp.where(here & reach == 0, mine_first, theirs_first)
+        reach = 2 * reach
+    return grown
 
 
 def einsum_high(form, left, right):
@@ -129,7 +141,7 @@
         lax.all_gather(shards[4], "dp", axis=0, tiled=True),
         lax.all_gather(shards[5], "dp", axis=0, tiled=True),
         lax.all_gather(shards[6], "dp", axis=0, tiled=True),
-        lax.all_gather(shards[7], "dp", axis=0, tiled=True),
+        doubled_up(shards[7], "dp", 0),
         lax.all_gather(shards[8], "dp", axis=0, tiled=True),
         lax.all_gather(shards[9], "dp", axis=0, tiled=True),
     )

time: 3730 us -> 3940 us (1.056)
  blocking collectives: 177 us -> 531 us
  waiting for transfers between devices: 2680 us -> 2510 us
    all_gather x1, blocking collectives: 29.5 us -> 384 us  [body(): lax.all_gather(shards[1], 'dp', axis=0, tiled=True)]
    ppermute x0 -> x4, waiting for transfers between devices: none -> 190 us  [doubled_up(): theirs = lax.ppermute(grown, axis, [(d, d ^ reach) for d in range(ways)])]
    all_gather x1, waiting for transfers between devices: 132 us -> 0.01 us  [body(): lax.all_gather(shards[9], 'dp', axis=0, tiled=True)]
    all_gather x1, waiting for transfers between devices: 132 us -> 0.02 us  [body(): lax.all_gather(shards[8], 'dp', axis=0, tiled=True)]
    all_gather x1, waiting for transfers between devices: 134 us -> 40.8 us  [body(): lax.all_gather(shards[7], 'dp', axis=0, tiled=True)]
  transfers between devices with their start and end apart: 18 -> 22, of which waited for: 13 -> 14; matrix products, arithmetic and copies ran while one was open for 9% -> 10% of each run, Pallas kernels for 0% -> 0%
where the time goes in v1:
time: 3940 us; the launch traced here: 3930 us
  waiting for transfers between devices  2510 us (64%)
  matrix products  594 us (15%)
  blocking collectives  531 us (13%)
  other arithmetic  129 us (3%)
  local copies, waits for them, and re-layouts  127 us (3%)
    reduce_scatter x1, waiting for transfers between devices, body(): lax.psum_scatter(grad_down, 'dp', scatter_dimension=0, tiled=True)  483 us
    reduce_scatter x1, waiting for transfers between devices, body(): lax.psum_scatter(grad_up, 'dp', scatter_dimension=0, tiled=True)  483 us
    reduce_scatter x1, waiting for transfers between devices, body(): lax.psum_scatter(grad_gate, 'dp', scatter_dimension=0, tiled=True)  482 us
    dot_general x104, matrix products, einsum_high(): return jnp.einsum(form, left, right, precision=lax.Precision.HIGHEST)  406 us
    all_gather x1, blocking collectives, body(): lax.all_gather(shards[1], 'dp', axis=0, tiled=True)  384 us
    ppermute x4, waiting for transfers between devices, doubled_up(): theirs = lax.ppermute(grown, axis, [(d, d ^ reach) for d in range(ways)])  190 us
    reduce_scatter x1, waiting for transfers between devices, body(): lax.psum_scatter(grad_key, 'dp', scatter_dimension=0, tiled=True)  184 us
    reduce_scatter x1, waiting for transfers between devices, body(): lax.psum_scatter(grad_value, 'dp', scatter_dimension=0, tiled=True)  183 us
  transfers between devices with their start and end apart: 22, of which 14 were waited for; matrix products, arithmetic and copies ran while one was open for 10% of the time, Pallas kernels for 0%

profile of v1, /device:TPU:10, one launch (start us, length us, event | category | flops | bytes accessed | tf_op | source)
XLA Modules:
  0.0 3934.6 jit_solution(2170725380270090385)
XLA Ops:
  14.0 35.8 all_gather.38
  49.8 40.5 %all-gather = bf16[16,1,128]{2,1,0:T(2,128)(2,1)S(1)} all-gather(bf16[1,1,128]{2,1,0:T(2,128)(2,1)S(1)} %bitcast.436), channel_id=1, replica_groups=mesh['dp'=16,'head'=2] {'dp'}, dimensions={0}, use_global_device_ids=true | all-gather | bytes 4352 | tf_op jit(solution)/shard_map/all_gather | solution.py:137
  110.8 57.6 %all-gather.12.cloned.1.call-done = bf16[2048,1024]{1,0:T(8,128)(2,1)} async-done(((bf16[128,1024]{1,0:T(8,128)(2,1)}), bf16[2048,1024]{1,0:T(8,128)(2,1)}) %all-gather.12.cloned.1.call-update) | async-done | bytes 4194320 | tf_op jit(solution)/shard_map/all_gather | solution.py:141
  181.9 64.0 %all-gather.14.cloned.1.call-done = bf16[2048,1024]{1,0:T(8,128)(2,1)} async-done(((bf16[128,1024]{1,0:T(8,128)(2,1)}), bf16[2048,1024]{1,0:T(8,128)(2,1)}) %all-gather.14.cloned.1.call-update) | async-done | bytes 4194320 | tf_op jit(solution)/shard_map/all_gather | solution.py:139
  260.2 175.8 %while.48 = (s32[]{:T(128)}, f32[4,64,512]{2,1,0:T(8,128)S(1)}, f32[4,64,512]{2,1,0:T(8,128)S(1)}, bf16[4,4,64,512]{3,2,0,1:T(8,128)(2,1)}, f32[4,4,64,512]{3,2,...) while((s32[]{:T(128)}, f32[4,64,512]{2,1,0:T(8,128)S(1)}, ...), condition=%wide.region_6.7_spmd.clone.clone, body=%wide.region_2.6_spmd.clone.clone.sunk | while | flops 640237632 | bytes 21779780 | solution.py:86
  284.2 15.7 fusion.412
  328.0 15.7 fusion.412
  371.8 15.7 fusion.412
  415.6 15.7 fusion.412
  448.3 16.3 collective-permute-done
  467.7 35.7 collective-permute-done.1
  507.3 137.8 %collective-permute-done.2 = bf16[512,2816]{1,0:T(8,128)(2,1)} collective-permute-done((bf16[512,2816]{1,0:T(8,128)(2,1)}, bf16[512,2816]{1,0:T(8,128)(2,1)}, u32[]{:S(2)}, u32[]{:S(2)}) %collective-permute-start.2) | collective-permute-done | bytes 2883616 | tf_op jit(solution)/shard_map/ppermute | solution.py:15
  665.8 383.6 %all-gather.1 = bf16[16,1,128]{2,1,0:T(2,128)(2,1)S(1)} all-gather(bf16[1,1,128]{2,1,0:T(2,128)(2,1)S(1)} %bitcast.437), channel_id=1, replica_groups=mesh['dp'=16,'head'=2] {'dp'}, dimensions={0}, use_global_device_ids=true | all-gather | bytes 4352 | tf_op jit(solution)/shard_map/all_gather | solution.py:138
  1079.7 18.9 multiply_convert_fusion
  1098.5 40.8 %all-gather.22.cloned.1.call-done = bf16[2048,2816]{1,0:T(8,128)(2,1)} async-done(((bf16[128,2816]{1,0:T(8,128)(2,1)}), bf16[2048,2816]{1,0:T(8,128)(2,1)}) %all-gather.22.cloned.1.call-update) | async-done | bytes 11534352 | tf_op jit(solution)/shard_map/all_gather | solution.py:185
  1171.5 17.4 all-reduce.11.cloned.1.call-done
  1212.9 388.9 %while.47 = (s32[]{:T(128)}, f32[4,64,512]{2,1,0:T(8,128)S(1)}, f32[4,64,512]{2,1,0:T(8,128)}, f32[4,4,64,512]{3,2,0,1:T(8,128)}, f32[4,4,64,512]{3,2,0,1:T(8,12...) while((s32[]{:T(128)}, f32[4,64,512]{2,1,0:T(8,128)S(1)}, ...), condition=%wide.region_24.25_spmd.clone, body=%wide.region_12.24_spmd.clone.sunk | while | flops 1495470592 | bytes 52910904 | solution.py:86
  1260.8 15.4 fusion.386
  1280.5 14.9 fusion.391
  1356.0 15.4 fusion.386
  1451.4 15.4 fusion.386
  1471.1 15.1 fusion.391
  1546.8 15.4 fusion.386
  1566.4 14.9 fusion.391
  1709.5 71.6 %all-reduce.3 = (f32[2048]{0:T(1024)S(1)}, f32[2048]{0:T(1024)S(1)}) all-reduce(f32[2048]{0:T(1024)S(1)} %get-tuple-element.678, f32[2048]{0:T(1024)S(1)} %copy-done.50), channel_id=2, replica_groups=mesh['dp'=16,'head'=2] {'dp'}, use_global_device_ids=true, to_apply=%region_28.29.clone | all-reduce | flops 4096 | bytes 32768
  1791.8 138.4 %reduce-scatter.9.cloned.1.call-done = f32[128,1024]{1,0:T(8,128)} async-done(((f32[2048,1024]{1,0:T(8,128)}), f32[128,1024]{1,0:T(8,128)}) %reduce-scatter.9.cloned.1.call-update) | async-done | bytes 524304 | tf_op jit(solution)/shard_map/reduce_scatter | solution.py:226
  1930.2 184.0 %reduce-scatter.11.cloned.1.call-done = f32[128,1024]{1,0:T(8,128)} async-done(((f32[2048,1024]{1,0:T(8,128)}), f32[128,1024]{1,0:T(8,128)}) %reduce-scatter.11.cloned.1.call-update) | async-done | bytes 524304 | tf_op jit(solution)/shard_map/reduce_scatter | solution.py:227
  2114.2 183.1 %reduce-scatter.13.cloned.1.call-done = f32[128,1024]{1,0:T(8,128)} async-done(((f32[2048,1024]{1,0:T(8,128)}), f32[128,1024]{1,0:T(8,128)}) %reduce-scatter.13.cloned.1.call-update) | async-done | bytes 524304 | tf_op jit(solution)/shard_map/reduce_scatter | solution.py:228
  2297.3 183.1 %reduce-scatter.17.cloned.1.call-done = f32[128,1024]{1,0:T(8,128)} async-done(((f32[2048,1024]{1,0:T(8,128)}), f32[128,1024]{1,0:T(8,128)}) %reduce-scatter.17.cloned.1.call-update) | async-done | bytes 524304 | tf_op jit(solution)/shard_map/reduce_scatter | solution.py:230
  2480.4 482.0 %reduce-scatter.19.cloned.1.call-done = f32[128,2816]{1,0:T(8,128)} async-done(((f32[2048,2816]{1,0:T(8,128)}), f32[128,2816]{1,0:T(8,128)}) %reduce-scatter.19.cloned.1.call-update) | async-done | bytes 1441808 | tf_op jit(solution)/shard_map/reduce_scatter | solution.py:231
  2962.3 482.6 %reduce-scatter.21.cloned.1.call-done = f32[128,2816]{1,0:T(8,128)} async-done(((f32[2048,2816]{1,0:T(8,128)}), f32[128,2816]{1,0:T(8,128)}) %reduce-scatter.21.cloned.1.call-update) | async-done | bytes 1441808 | tf_op jit(solution)/shard_map/reduce_scatter | solution.py:232
  3445.0 482.6 %reduce-scatter.23.cloned.1.call-done = f32[128,2816]{1,0:T(8,128)} async-done(((f32[2048,2816]{1,0:T(8,128)}), f32[128,2816]{1,0:T(8,128)}) %reduce-scatter.23.cloned.1.call-update) | async-done | bytes 1441808 | tf_op jit(solution)/shard_map/reduce_scatter | solution.py:233
  (693 shorter events, 680.2 us)
Async XLA Ops:
  7.2 42.6 %copy-start.57 = (bf16[128]{0:T(256)(128)(2,1)S(1)}, bf16[128]{0:T(256)(128)(2,1)}, u32[]{:S(2)}) copy-start(bf16[128]{0:T(256)(128)(2,1)} %param.21) | copy-start | bytes 772
  7.2 83.1 %copy-start.5 = (bf16[512,2048]{1,0:T(8,128)(2,1)S(1)}, bf16[512,2048]{1,0:T(8,128)(2,1)}, u32[]{:S(2)}) copy-start(bf16[512,2048]{1,0:T(8,128)(2,1)} %param.18) | copy-start | bytes 6291460
  7.2 89.1 %all-gather.10.cloned.1.call-start = ((), (), s32[]{:S(2)}) async-start(), calls=%async_computation.8 | async-start | bytes 4456448 | tf_op jit(solution)/shard_map/all_gather | solution.py:140
  7.9 160.5 %all-gather.12.cloned.1.call-start = ((), (), s32[]{:S(2)}) async-start(), calls=%async_computation.9 | async-start | bytes 4456448 | tf_op jit(solution)/shard_map/all_gather | solution.py:141
  8.7 237.2 %all-gather.14.cloned.1.call-start = ((), (), s32[]{:S(2)}) async-start(), calls=%async_computation.10 | async-start | bytes 4456448 | tf_op jit(solution)/shard_map/all_gather | solution.py:139
  9.4 429.2 %all-gather.16.cloned.1.call-start = ((), (), s32[]{:S(2)}) async-start(), calls=%async_computation.11 | async-start | bytes 4456448 | tf_op jit(solution)/shard_map/all_gather | solution.py:143
  10.0 1039.6 %all-reduce.9.cloned.1.call-start = ((), (), s32[]{:S(2)}) async-start(), calls=%async_computation.12 | async-start | bytes 8388608 | tf_op jit(solution)/shard_map/psum | solution.py:167
  49.8 41.0 %copy-start.37 = (bf16[2048,128]{1,0:T(8,128)(2,1)}, bf16[2048,128]{1,0:T(8,128)(2,1)S(1)}, u32[]{:S(2)}) copy-start(bf16[2048,128]{1,0:T(8,128)(2,1)S(1)} %all_gather.38) | copy-start | bytes 1572868
  90.3 155.6 %copy-start.47 = (f32[16,1,128]{2,1,0:T(1,128)}, f32[16,1,128]{2,1,0:T(1,128)S(1)}, u32[]{:S(2)}) copy-start(f32[16,1,128]{2,1,0:T(1,128)S(1)} %convert_element_type.104) | copy-start | bytes 24580
  90.8 155.1 %copy-start.51 = (f32[512]{0:T(512)}, f32[512]{0:T(512)S(1)}, u32[]{:S(2)}) copy-start(f32[512]{0:T(512)S(1)} %fusion.158) | copy-start | bytes 6148
  445.6 609.3 %all-gather.18.cloned.1.call-start = ((), (), s32[]{:S(2)}) async-start(), calls=%async_computation.13 | async-start | bytes 12255232 | tf_op jit(solution)/shard_map/all_gather | solution.py:145
  446.1 620.6 %all-gather.20.cloned.1.call-start = ((), (), s32[]{:S(2)}) async-start(), calls=%async_computation.14 | async-start | bytes 12255232 | tf_op jit(solution)/shard_map/all_gather | solution.py:146
  446.9 692.5 %all-gather.22.cloned.1.call-start = ((), (), s32[]{:S(2)}) async-start(), calls=%async_computation.15 | async-start | bytes 12255232 | tf_op jit(solution)/shard_map/all_gather | solution.py:185
  447.6 741.3 %all-reduce.11.cloned.1.call-start = ((), (), s32[]{:S(2)}) async-start(), calls=%async_computation.16 | async-start | bytes 8388608 | tf_op jit(solution)/shard_map/psum | solution.py:199
  447.7 17.0 collective-permute-start
  467.1 36.4 collective-permute-start.1
  506.8 138.2 %collective-permute-start.2 = (bf16[512,2816]{1,0:T(8,128)(2,1)}, bf16[512,2816]{1,0:T(8,128)(2,1)}, u32[]{:S(2)}, u32[]{:S(2)}) collective-permute-start(bf16[512,2816]{1,0:T(8,128)(2,1)} %maximum_select_fusion.3), channel_id=1, source_target_pairs={{0,8},{2,10},{4,12},{6,14},{8,0},{10,2},{12,4},{14,6},{16,24},{18,... | collective-permute-start | bytes 8650760 | tf_op jit(solution)/shard_map/ppermute | solution.py:15
  507.3 158.5 %copy-start.58 = (bf16[128]{0:T(256)(128)(2,1)S(1)}, bf16[128]{0:T(256)(128)(2,1)}, u32[]{:S(2)}) copy-start(bf16[128]{0:T(256)(128)(2,1)} %param.22) | copy-start | bytes 772
  507.3 542.2 %copy-start.59 = (s32[2]{0:T(128)S(1)}, s32[2]{0:T(128)}, u32[]{:S(2)}) copy-start(s32[2]{0:T(128)} %param.20) | copy-start | bytes 28
  654.1 425.5 %collective-permute-start.3 = (bf16[1024,2816]{1,0:T(8,128)(2,1)}, bf16[1024,2816]{1,0:T(8,128)(2,1)}, u32[]{:S(2)}, u32[]{:S(2)}) collective-permute-start(bf16[1024,2816]{1,0:T(8,128)(2,1)} %maximum_select_fusion.2), channel_id=1, source_target_pairs={{0,16},{2,18},{4,20},{6,22},{8,24},{10,26},{12,28},{14,30},{16,0},... | collective-permute-start | bytes 17301512 | tf_op jit(solution)/shard_map/ppermute | solution.py:15
  1049.5 144.6 %copy-start.53 = (f32[512]{0:T(512)}, f32[512]{0:T(512)S(1)}, u32[]{:S(2)}) copy-start(f32[512]{0:T(512)S(1)} %and_convert_fusion) | copy-start | bytes 6148
  1054.9 24.8 copy-start.36
  1159.8 546.2 %all-reduce.13.cloned.1.call-start = ((), (), s32[]{:S(2)}) async-start(), calls=%async_computation.25 | async-start | bytes 16777216 | tf_op jit(solution)/shard_map/psum | solution.py:175
  1628.0 163.8 %reduce-scatter.15.cloned.1.call-start = ((), (), s32[]{:S(2)}) async-start(), calls=%async_computation.20 | async-start | bytes 1114112 | tf_op jit(solution)/shard_map/reduce_scatter | solution.py:229
  1631.6 298.5 %reduce-scatter.9.cloned.1.call-start = ((), (), s32[]{:S(2)}) async-start(), calls=%async_computation.17 | async-start | bytes 8912896 | tf_op jit(solution)/shard_map/reduce_scatter | solution.py:226
  1639.5 474.7 %reduce-scatter.11.cloned.1.call-start = ((), (), s32[]{:S(2)}) async-start(), calls=%async_computation.18 | async-start | bytes 8912896 | tf_op jit(solution)/shard_map/reduce_scatter | solution.py:227
  1645.7 651.5 %reduce-scatter.13.cloned.1.call-start = ((), (), s32[]{:S(2)}) async-start(), calls=%async_computation.19 | async-start | bytes 8912896 | tf_op jit(solution)/shard_map/reduce_scatter | solution.py:228
  1652.8 827.6 %reduce-scatter.17.cloned.1.call-start = ((), (), s32[]{:S(2)}) async-start(), calls=%async_computation.21 | async-start | bytes 8912896 | tf_op jit(solution)/shard_map/reduce_scatter | solution.py:230
  1663.1 1299.2 %reduce-scatter.19.cloned.1.call-start = ((), (), s32[]{:S(2)}) async-start(), calls=%async_computation.22 | async-start | bytes 24510464 | tf_op jit(solution)/shard_map/reduce_scatter | solution.py:231
  1676.8 1768.1 %reduce-scatter.21.cloned.1.call-start = ((), (), s32[]{:S(2)}) async-start(), calls=%async_computation.23 | async-start | bytes 24510464 | tf_op jit(solution)/shard_map/reduce_scatter | solution.py:232
  1690.0 2237.6 %reduce-scatter.23.cloned.1.call-start = ((), (), s32[]{:S(2)}) async-start(), calls=%async_computation.24 | async-start | bytes 24510464 | tf_op jit(solution)/shard_map/reduce_scatter | solution.py:233
  1704.1 78.2 %copy-start.56 = (f32[512]{0:T(512)S(1)}, f32[512]{0:T(512)}, u32[]{:S(2)}) copy-start(f32[512]{0:T(512)} %copy-done.55) | copy-start | bytes 6148
  (134 other events, 1036.0 us)
Sparse Core Ops, SparseCore 0:
  10.8 80.0 all-gather.9
  93.6 74.7 all-gather.11
  171.2 74.6 all-gather.13
  248.5 74.6 all-gather.15
  445.7 27.4 all-reduce.8
  476.1 193.7 all-gather.17
  673.0 290.2 all-gather.19
  966.5 172.8 all-gather.21
  1159.9 28.9 all-reduce.10
  1628.2 40.1 all-reduce.12
  1671.2 68.0 reduce-scatter.14
  1742.1 188.0 reduce-scatter.8
  1933.1 181.0 reduce-scatter.10
  2117.0 180.2 reduce-scatter.12
  2300.1 180.2 reduce-scatter.16
  2483.2 479.0 reduce-scatter.18
  2965.2 479.7 reduce-scatter.20
  3447.8 479.7 reduce-scatter.22
